TPU v7x, 128 devices: a whole 4x4x4 slice. The times are simulated.
128 devices in a mesh: expert: 64 (over x, y, z), dp: 2 (over core).
Axes of the slice: x: 4, y: 4, z: 4, core: 2. Of those that a mesh axis runs over, the one named last changes fastest.
Arguments:
- tokens: bfloat16 [12288, 4096], P(('expert', 'dp')), may hold values from -6 to 6
- w_gate: bfloat16 [128, 4096, 768], P(('expert', 'dp')), may hold values from -0.09375 to 0.09375
- w_up: bfloat16 [128, 4096, 768], P(('expert', 'dp')), may hold values from -0.09375 to 0.09375
- w_down: bfloat16 [128, 768, 4096], P(('expert', 'dp')), may hold values from -0.21875 to 0.21875
- route_ids: int32 [12288, 8], P(('expert', 'dp')), may hold values from 0 to 127, all different within a row
- route_gates: float32 [12288, 8], P(('expert', 'dp')), may hold values from 0.05 to 0.4
- hot_experts: int32 [1], replicated, may hold values from 0 to 127
Outputs:
- mixed: bfloat16 [12288, 4096], P(('expert', 'dp'))
Inputs may be any that keep to these rules, and one draw needn't show every extreme that they name: `route_ids`: each row names 8 different experts.
All inputs are finite; a program needn't handle non-finite values.
Results may differ from a plain program's by a relative error of at most 0.007.
Values may be sent and summed in bfloat16 or wider, within the bound.
A program may use at most 192 MiB of HBM per device.

v0:
```python
import jax
import jax.numpy as jnp
from jax import lax
from jax.sharding import PartitionSpec as P

CAP = 6


def expert_ffn(in_rows, gate_w, up_w, down_w):
    gate_val = jnp.dot(in_rows, gate_w, preferred_element_type=jnp.float32)
    up_val = jnp.dot(in_rows, up_w, preferred_element_type=jnp.float32)
    hidden = (jax.nn.silu(gate_val) * up_val).astype(jnp.bfloat16)
    return jnp.dot(hidden, down_w, preferred_element_type=jnp.float32).astype(jnp.bfloat16)


def on_device(tokens, w_gate, w_up, w_down, route_ids, route_gates, hot_experts):
    feat_width = tokens.shape[1]
    tok_rows = tokens.shape[0]
    top_k = route_ids.shape[1]
    n_dp = lax.axis_size("dp")
    experts = lax.axis_size("expert") * n_dp
    hot_id = hot_experts[0]
    me = lax.axis_index("expert") * n_dp + lax.axis_index("dp")
    own = (w_gate[0], w_up[0], w_down[0])
    with jax.named_scope("hot_weight_broadcast"):
        is_root = me == hot_id
        hot_w = tuple(
            (lax.psum(jnp.where(is_root, w, jnp.zeros_like(w)), ("expert", "dp")) for w in own)
        )
    with jax.named_scope("routing"):
        flat_ids = route_ids.reshape(-1)
        labels = lax.iota(jnp.int32, experts)
        onehot = (flat_ids[:, None] == labels[None, :]).astype(jnp.int32)
        rank_of = jnp.sum(onehot * (jnp.cumsum(onehot, axis=0) - 1), axis=1)
        is_kept = (flat_ids != hot_id) & (rank_of < CAP)
        slot_of = jnp.where(is_kept, flat_ids * CAP + rank_of, experts * CAP)
        slots = lax.iota(jnp.int32, experts * CAP)
        hit = slot_of[None, :] == slots[:, None]
        dispatch = jnp.any(hit.reshape(experts * CAP, tok_rows, top_k), axis=2)
    with jax.named_scope("dispatch"):
        outgoing = jnp.dot(
            dispatch.astype(tokens.dtype), tokens, preferred_element_type=jnp.float32
        ).astype(tokens.dtype)
        to_send = outgoing.reshape(experts, CAP * feat_width)
        arrived = lax.all_to_all(to_send, ("expert", "dp"), 0, 0, tiled=True)
    with jax.named_scope("expert_ffn"):
        results = expert_ffn(arrived.reshape(-1, feat_width), *own)
    with jax.named_scope("return"):
        come_back = lax.all_to_all(
            results.reshape(experts, CAP * feat_width), ("expert", "dp"), 0, 0, tiled=True
        )
        returned = come_back.reshape(experts * CAP, feat_width)
    with jax.named_scope("combine"):
        gate_flat = route_gates.reshape(-1)
        cold_weight = jnp.where(is_kept, gate_flat, jnp.zeros_like(gate_flat))
        weight_of_slot = jnp.where(hit, cold_weight[None, :], 0.0)
        combine = jnp.sum(weight_of_slot.reshape(experts * CAP, tok_rows, top_k), axis=2).T
        cold_sum = jnp.dot(
            combine,
            returned.astype(jnp.float32),
            precision=lax.Precision.HIGHEST,
            preferred_element_type=jnp.float32,
        )
    with jax.named_scope("hot_expert"):
        hot_out = expert_ffn(tokens, *hot_w)
        hot_weight = jnp.sum(
            jnp.where(route_ids == hot_id, route_gates, jnp.zeros_like(route_gates)), axis=1
        )
        combined = cold_sum + hot_weight[:, None] * hot_out.astype(jnp.float32)
    return combined.astype(jnp.bfloat16)


def solution(mesh):
    in_specs = (
        P(("expert", "dp"), None),
        P(("expert", "dp"), None, None),
        P(("expert", "dp"), None, None),
        P(("expert", "dp"), None, None),
        P(("expert", "dp"), None),
        P(("expert", "dp"), None),
        P(),
    )
    out_specs = P(("expert", "dp"), None)
    return jax.shard_map(
        on_device, mesh=mesh, in_specs=in_specs, out_specs=out_specs, check_vma=False
    )
```

profile of v0, /device:TPU:0, one launch (start us, length us, event | category | flops | bytes accessed | tf_op | source)
XLA Modules:
  0.0 559.9 jit_solution(3620452224844530923)
XLA Ops:
  6.5 0.9 copy.64
  8.3 0.2 fusion.13
  8.7 0.3 fusion.15
  9.2 0.7 add_select_fusion
  10.0 0.8 fusion.8
  10.8 4.5 convolution_convert_fusion
  15.2 23.8 %all_to_all.16 = bf16[128,1,24576]{2,1,0:T(2,128)(2,1)} reshape(bf16[768,4096]{1,0:T(8,128)(2,1)} %convolution_convert_fusion) | data formatting | bytes 12582912 | tf_op jit(solution)/shard_map/dispatch/all_to_all | solution.py:45
  39.0 0.5 broadcast.85
  39.4 38.9 %reduce.2 = bf16[128,24576]{1,0:T(8,128)(2,1)} reduce(bf16[128,1,24576]{2,1,0:T(2,128)(2,1)} %all_to_all.16, bf16[]{:T(256)} %broadcast.85), dimensions={1}, to_apply=%all_to_all.16.reduce_sub_computation | reduce | bytes 12582914 | tf_op jit(solution)/shard_map/dispatch/all_to_all | solution.py:45
  78.3 9.4 %reshape.90 = bf16[128,2,12288]{2,1,0:T(2,128)(2,1)} reshape(bf16[128,24576]{1,0:T(8,128)(2,1)} %reduce.2) | data formatting | bytes 12582912
  87.7 11.6 %all-to-all-start = ((bf16[128,2,12288]{2,1,0:T(2,128)(2,1)}), bf16[128,2,12288]{2,1,0:T(2,128)(2,1)}, u32[]{:S(2)}, u32[]{:S(2)}) async-start(bf16[128,2,12288]{2,1,0:T(2,128)(2,1)} %reshape.90), calls=%async_computation | async-start | bytes 12582912 | tf_op jit(solution)/shard_map/dispatch/all_to_all | solution.py:45
  99.4 5.9 %bitcast_select_fusion = bf16[768,4096]{1,0:T(8,128)(2,1)} fusion(bf16[1,768,4096]{2,1,0:T(8,128)(2,1)} %param.10, pred[]{:T(512)S(6)} %eq.59), kind=kLoop, calls=%fused_computation.2 | loop fusion | flops 3145728 | bytes 12582913 | tf_op jit(solution)/shard_map/hot_weight_broadcast/jit(_where)/select_n | solution.py:28
  105.3 9.9 %bitcast_select_fusion.1 = (bf16[4096,768]{1,0:T(8,128)(2,1)}, bf16[4096,768]{1,0:T(8,128)(2,1)}) fusion(bf16[1,4096,768]{2,1,0:T(8,128)(2,1)} %param.9, pred[]{:T(512)S(6)} %eq.59, bf16[1,4096,768]{2,1,0:T(8,128)(2,1)} %param.8), kind=kLoop, calls=%fused_computation.4 | loop fusion | flops 6291456 | bytes 25165824 | tf_op jit(solution)/shard_map/hot_weight_broadcast/jit(_where)/select_n | solution.py:28
  115.1 65.2 %all-to-all-done = bf16[128,2,12288]{2,1,0:T(2,128)(2,1)} async-done(((bf16[128,2,12288]{2,1,0:T(2,128)(2,1)}), bf16[128,2,12288]{2,1,0:T(2,128)(2,1)}, u32[]{:S(2)}, u32[]{:S(2)}) %all-to-all-start) | async-done | bytes 6291488 | tf_op jit(solution)/shard_map/dispatch/all_to_all | solution.py:45
  180.4 34.5 %reshape.91 = bf16[128,1,24576]{2,1,0:T(2,128)(2,1)} reshape(bf16[128,2,12288]{2,1,0:T(2,128)(2,1)} %all-to-all-done) | data formatting | bytes 12582912
  214.8 38.3 %reduce = bf16[128,24576]{1,0:T(8,128)(2,1)} reduce(bf16[128,1,24576]{2,1,0:T(2,128)(2,1)} %reshape.91, bf16[]{:T(256)} %constant.43), dimensions={1}, to_apply=%all_to_all.13.reduce_sub_computation | reduce | bytes 12582914 | tf_op jit(solution)/shard_map/dispatch/all_to_all | solution.py:45
  253.2 11.2 %reshape.86 = bf16[768,4096]{1,0:T(8,128)(2,1)} reshape(bf16[128,24576]{1,0:T(8,128)(2,1)} %reduce) | data formatting | bytes 12582912 | tf_op jit(solution)/shard_map/expert_ffn/reshape | solution.py:47
  264.4 9.1 %fusion.3 = f32[768,768]{1,0:T(8,128)S(1)} fusion(bf16[768,4096]{1,0:T(8,128)(2,1)} %reshape.86, bf16[1,4096,768]{2,1,0:T(8,128)(2,1)} %param.8), kind=kOutput, calls=%fused_computation.8 | convolution fusion | flops 4831838208 | bytes 14942208 | tf_op jit(solution)/shard_map/expert_ffn/dot_general | solution.py:10
  273.5 8.0 %multiply_convert_fusion = bf16[768,768]{1,0:T(8,128)(2,1)S(1)} fusion(f32[768,768]{1,0:T(8,128)S(1)} %fusion.3, bf16[768,4096]{1,0:T(8,128)(2,1)S(1)} %copy-done.1, bf16[1,4096,768]{2,1,0:T(8,128)(2,1)} %param.9), kind=kOutput, calls=%fused_computation.15 | convolution fusion | flops 4835377152 | bytes 16121856 | tf_op jit(solution)/shard_map/expert_ffn/dot_general | solution.py:11
  281.6 7.1 %convolution_convert_fusion.1 = bf16[768,4096]{1,0:T(8,128)(2,1)} fusion(bf16[768,768]{1,0:T(8,128)(2,1)S(1)} %multiply_convert_fusion, bf16[1,768,4096]{2,1,0:T(8,128)(2,1)S(1)} %bitcast.50), kind=kOutput, calls=%fused_computation.1 | convolution fusion | flops 4834983936 | bytes 13762560 | tf_op jit(solution)/shard_map/expert_ffn/dot_general | solution.py:13
  288.7 23.9 %all_to_all.17 = bf16[128,1,24576]{2,1,0:T(2,128)(2,1)} reshape(bf16[768,4096]{1,0:T(8,128)(2,1)} %convolution_convert_fusion.1) | data formatting | bytes 12582912 | tf_op jit(solution)/shard_map/return/all_to_all | solution.py:49
  312.5 38.8 %reduce.3 = bf16[128,24576]{1,0:T(8,128)(2,1)} reduce(bf16[128,1,24576]{2,1,0:T(2,128)(2,1)} %all_to_all.17, bf16[]{:T(256)} %broadcast.85), dimensions={1}, to_apply=%all_to_all.17.reduce_sub_computation | reduce | bytes 12582914 | tf_op jit(solution)/shard_map/return/all_to_all | solution.py:49
  351.4 9.7 %reshape.92 = bf16[128,2,12288]{2,1,0:T(2,128)(2,1)} reshape(bf16[128,24576]{1,0:T(8,128)(2,1)} %reduce.3) | data formatting | bytes 12582912
  361.1 7.8 %all-to-all-start.1 = ((bf16[128,2,12288]{2,1,0:T(2,128)(2,1)}), bf16[128,2,12288]{2,1,0:T(2,128)(2,1)}, u32[]{:S(2)}, u32[]{:S(2)}) async-start(bf16[128,2,12288]{2,1,0:T(2,128)(2,1)} %reshape.92), calls=%async_computation.1 | async-start | bytes 12582912 | tf_op jit(solution)/shard_map/return/all_to_all | solution.py:49
  369.0 0.8 select_reduce_fusion
  369.8 81.9 %all-reduce.3.cloned.1.call-done = (bf16[768,4096]{1,0:T(8,128)(2,1)}, bf16[4096,768]{1,0:T(8,128)(2,1)}, bf16[4096,768]{1,0:T(8,128)(2,1)}) async-done(((bf16[768,4096]{1,0:T(8,128)(2,1)}, bf16[4096,768]{1,0:T(8,128)(2,1)}, bf16[4096,768]{1,0:T(8,128)(2,1)}), (bf16[768,4096]{1,0:T(8,128)(2,1)}, bf16[4096,768]{1,0:T(8,128)(2,1)}, bf16[4096,768]{1,0:T(8,128)(2,1)})) %all-reduce.3.cloned.1.call-update) | async-done | bytes 18874384 | tf_op jit(solution)/shard_map/hot_weight_broadcast/psum | solution.py:28
  451.7 3.9 convolution_bitcast_fusion.1
  455.6 7.1 %fusion.7 = f32[96,4096]{1,0:T(8,128)S(1)} fusion(bf16[768,4096]{1,0:T(8,128)(2,1)} %get-tuple-element.5, bf16[96,4096]{1,0:T(8,128)(2,1)S(1)} %copy-done, bf16[4096,768]{1,0:T(8,128)(2,1)} %get-tuple-element.6, f32[96]{0:T(128)S(1)} %get-tuple-element.9, f32[96,768]{1,0:T(8,128)S(1)} %convolution_bitcast_fusion.1), kind=kOutput, calls=%fused_computation.14 | convolution fusion | flops 1209581568 | bytes 15237504 | tf_op jit(solution)/shard_map/hot_expert/dot_general | solution.py:13
  462.8 33.8 %reshape.93 = bf16[128,1,24576]{2,1,0:T(2,128)(2,1)} reshape(bf16[128,2,12288]{2,1,0:T(2,128)(2,1)} %all-to-all-done.1) | data formatting | bytes 12582912
  496.6 38.3 %reduce.1 = bf16[128,24576]{1,0:T(8,128)(2,1)} reduce(bf16[128,1,24576]{2,1,0:T(2,128)(2,1)} %reshape.93, bf16[]{:T(256)} %constant.43), dimensions={1}, to_apply=%all_to_all.15.reduce_sub_computation | reduce | bytes 12582914 | tf_op jit(solution)/shard_map/return/all_to_all | solution.py:49
  534.9 11.1 %reshape.87 = bf16[768,4096]{1,0:T(8,128)(2,1)} reshape(bf16[128,24576]{1,0:T(8,128)(2,1)} %reduce.1) | data formatting | bytes 12582912 | tf_op jit(solution)/shard_map/return/reshape | solution.py:52
  546.0 6.8 %fusion.5 = bf16[96,4096]{1,0:T(8,128)(2,1)} fusion(f32[96,4096]{1,0:T(8,128)S(1)} %fusion.7, f32[768,96]{0,1:T(8,128)S(1)} %select_reduce_fusion, bf16[768,4096]{1,0:T(8,128)(2,1)} %reshape.87), kind=kOutput, calls=%fused_computation.11 | convolution fusion | flops 3624665088 | bytes 8945664 | tf_op jit(solution)/shard_map/combine/dot_general | solution.py:58
  (28 shorter events, 0.9 us)
Async XLA Ops:
  6.5 4.2 copy-start
  87.7 92.7 %all-to-all-start = ((bf16[128,2,12288]{2,1,0:T(2,128)(2,1)}), bf16[128,2,12288]{2,1,0:T(2,128)(2,1)}, u32[]{:S(2)}, u32[]{:S(2)}) async-start(bf16[128,2,12288]{2,1,0:T(2,128)(2,1)} %reshape.90), calls=%async_computation | async-start | bytes 12582912 | tf_op jit(solution)/shard_map/dispatch/all_to_all | solution.py:45
  99.3 352.4 %all-reduce.3.cloned.1.call-start = ((), (), s32[]{:S(2)}) async-start(), calls=%async_computation.2 | async-start | bytes 37748736 | tf_op jit(solution)/shard_map/hot_weight_broadcast/psum | solution.py:28
  253.2 28.4 %slice-start = ((s8[6291456]{0:T(1024)(128)(4,1)}), s8[2097152]{0:T(1024)(128)(4,1)S(1)}, s32[]{:S(2)}) async-start(s8[6291456]{0:T(1024)(128)(4,1)} %bitcast.49), calls=%async_computation.3 | async-start | bytes 4194304
  264.4 9.1 %copy-start.1 = (bf16[768,4096]{1,0:T(8,128)(2,1)S(1)}, bf16[768,4096]{1,0:T(8,128)(2,1)}, u32[]{:S(2)}) copy-start(bf16[768,4096]{1,0:T(8,128)(2,1)} %reshape.86) | copy-start | bytes 18874372
  264.4 17.2 %slice-start.1 = ((s8[6291456]{0:T(1024)(128)(4,1)}), s8[4194304]{0:T(1024)(128)(4,1)S(1)}, s32[]{:S(2)}) async-start(s8[6291456]{0:T(1024)(128)(4,1)} %bitcast.49), calls=%async_computation.4 | async-start | bytes 8388608
  361.1 7.8 %copy-start.2 = (s32[96,8]{0,1:T(8,128)S(1)}, s32[96,8]{0,1:T(8,128)}, u32[]{:S(2)}) copy-start(s32[96,8]{0,1:T(8,128)} %param.11) | copy-start | bytes 9220
  361.1 7.8 %copy-start.3 = (f32[96,8]{0,1:T(8,128)S(1)}, f32[96,8]{0,1:T(8,128)}, u32[]{:S(2)}) copy-start(f32[96,8]{0,1:T(8,128)} %param.12) | copy-start | bytes 9220
  361.1 101.7 %all-to-all-start.1 = ((bf16[128,2,12288]{2,1,0:T(2,128)(2,1)}), bf16[128,2,12288]{2,1,0:T(2,128)(2,1)}, u32[]{:S(2)}, u32[]{:S(2)}) async-start(bf16[128,2,12288]{2,1,0:T(2,128)(2,1)} %reshape.92), calls=%async_computation.1 | async-start | bytes 12582912 | tf_op jit(solution)/shard_map/return/all_to_all | solution.py:49
Sparse Core Ops, SparseCore 0:
  115.3 336.3 all-reduce.2
where the time goes:
time: 571 us; the launch traced here: 560 us
  other arithmetic  173 us (30%)
  local copies, waits for them, and re-layouts  159 us (28%)
  waiting for transfers between devices  147 us (26%)
  matrix products  46.5 us (8%)
  starting transfers between devices  19.5 us (3%)
  between operations  14.5 us (3%)
    unnamed x17, local copies, waits for them, and re-layouts  88.2 us
    psum x1, waiting for transfers between devices, on_device(): lax.psum(jnp.where(is_root, w, jnp.zeros_like(w)), ('expert', 'dp'))  81.9 us
    all_to_all x2, other arithmetic, on_device(): arrived = lax.all_to_all(to_send, ('expert', 'dp'), 0, 0, tiled=True)  77.2 us
    all_to_all x2, other arithmetic, on_device(): lax.all_to_all(results.reshape(experts, CAP * feat_width), ('expert', 'dp...  77.2 us
    all_to_all x1, waiting for transfers between devices, on_device(): arrived = lax.all_to_all(to_send, ('expert', 'dp'), 0, 0, tiled=True)  65.2 us
    all_to_all x2, local copies, waits for them, and re-layouts, on_device(): arrived = lax.all_to_all(to_send, ('expert', 'dp'), 0, 0, tiled=True)  24.2 us
    all_to_all x1, local copies, waits for them, and re-layouts, on_device(): lax.all_to_all(results.reshape(experts, CAP * feat_width), ('expert', 'dp...  23.9 us
    select_n x2, other arithmetic, on_device(): jnp.where(is_root, w, jnp.zeros_like(w))  15.8 us
  transfers between devices with their start and end apart: 3, of which 2 were waited for; matrix products, arithmetic and copies ran while one was open for 33% of the time, Pallas kernels for 0%

commit v1 on v0

--- a/solution.py
+++ b/solution.py
@@ -25,7 +25,10 @@
     with jax.named_scope("hot_weight_broadcast"):
         is_root = me == hot_id
         hot_w = tuple(
-            (lax.psum(jnp.where(is_root, w, jnp.zeros_like(w)), ("expert", "dp")) for w in own)
+            (
+                lax.psum(lax.psum(jnp.where(is_root, w, jnp.zeros_like(w)), "expert"), "dp")
+                for w in own
+            )
         )
     with jax.named_scope("routing"):
         flat_ids = route_ids.reshape(-1)

time: 571 us -> 798 us (1.40)
  waiting for transfers between devices: 147 us -> 304 us
  blocking collectives: 0 us -> 83.3 us
  starting transfers between devices: 19.5 us -> 6.95 us
    psum x1 -> x2, waiting for transfers between devices: 81.9 us -> 229 us  [the longest x1 229 us: on_device(): lax.psum(jnp.where(is_root, w, jnp.zeros_like(w)), 'expert')]
    all_to_all x0 -> x1, blocking collectives: none -> 83.3 us  [on_device(): arrived = lax.all_to_all(to_send, ('expert', 'dp'), 0, 0, tiled=True)]
    all_to_all x1, waiting for transfers between devices: 0.01 us -> 74.8 us  [on_device(): lax.all_to_all(results.reshape(experts, CAP * feat_width), ('expert', 'dp...]
    all_to_all x1 -> x0, waiting for transfers between devices: 65.2 us -> none  [on_device(): arrived = lax.all_to_all(to_send, ('expert', 'dp'), 0, 0, tiled=True)]
    all_to_all x1 -> x0, starting transfers between devices: 11.6 us -> none  [on_device(): arrived = lax.all_to_all(to_send, ('expert', 'dp'), 0, 0, tiled=True)]
  transfers between devices with their start and end apart: 3 -> 3, of which waited for: 2 -> 2; matrix products, arithmetic and copies ran while one was open for 33% -> 38% of each run, Pallas kernels for 0% -> 0%
where the time goes in v1:
time: 798 us; the launch traced here: 786 us
  waiting for transfers between devices  304 us (38%)
  other arithmetic  172 us (22%)
  local copies, waits for them, and re-layouts  159 us (20%)
  blocking collectives  83.3 us (10%)
  matrix products  46.5 us (6%)
  between operations  14.5 us (2%)
    psum x1, waiting for transfers between devices, on_device(): lax.psum(jnp.where(is_root, w, jnp.zeros_like(w)), 'expert')  229 us
    unnamed x17, local copies, waits for them, and re-layouts  87.1 us
    all_to_all x1, blocking collectives, on_device(): arrived = lax.all_to_all(to_send, ('expert', 'dp'), 0, 0, tiled=True)  83.3 us
    all_to_all x2, other arithmetic, on_device(): arrived = lax.all_to_all(to_send, ('expert', 'dp'), 0, 0, tiled=True)  77.1 us
    all_to_all x2, other arithmetic, on_device(): lax.all_to_all(results.reshape(experts, CAP * feat_width), ('expert', 'dp...  77.1 us
    all_to_all x1, waiting for transfers between devices, on_device(): lax.all_to_all(results.reshape(experts, CAP * feat_width), ('expert', 'dp...  74.8 us
    all_to_all x2, local copies, waits for them, and re-layouts, on_device(): arrived = lax.all_to_all(to_send, ('expert', 'dp'), 0, 0, tiled=True)  25.2 us
    all_to_all x1, local copies, waits for them, and re-layouts, on_device(): lax.all_to_all(results.reshape(experts, CAP * feat_width), ('expert', 'dp...  23.8 us
  transfers between devices with their start and end apart: 3, of which 2 were waited for; matrix products, arithmetic and copies ran while one was open for 38% of the time, Pallas kernels for 0%

profile of v1, /device:TPU:0, one launch (start us, length us, event | category | flops | bytes accessed | tf_op | source)
XLA Modules:
  0.0 786.3 jit_solution(15046526941626902069)
XLA Ops:
  7.3 5.9 bitcast_select_fusion
  13.1 10.0 %bitcast_select_fusion.1 = (bf16[4096,768]{1,0:T(8,128)(2,1)}, bf16[4096,768]{1,0:T(8,128)(2,1)}) fusion(bf16[1,4096,768]{2,1,0:T(8,128)(2,1)} %param.9, pred[]{:T(512)S(6)} %eq.59, bf16[1,4096,768]{2,1,0:T(8,128)(2,1)} %param.8), kind=kLoop, calls=%fused_computation.4 | loop fusion | flops 6291456 | bytes 25165824 | tf_op jit(solution)/shard_map/hot_weight_broadcast/jit(_where)/select_n | solution.py:29
  23.2 0.6 copy-done.2
  24.0 0.1 copy.66
  24.1 0.2 fusion.13
  24.4 228.8 %all-reduce.5.cloned.1.call-done = (bf16[768,4096]{1,0:T(8,128)(2,1)}, bf16[4096,768]{1,0:T(8,128)(2,1)}, bf16[4096,768]{1,0:T(8,128)(2,1)}) async-done(((bf16[768,4096]{1,0:T(8,128)(2,1)}, bf16[4096,768]{1,0:T(8,128)(2,1)}, bf16[4096,768]{1,0:T(8,128)(2,1)}), (bf16[768,4096]{1,0:T(8,128)(2,1)}, bf16[4096,768]{1,0:T(8,128)(2,1)}, bf16[4096,768]{1,0:T(8,128)(2,1)})) %all-reduce.5.cloned.1.call-update) | async-done | bytes 18874384 | tf_op jit(solution)/shard_map/hot_weight_broadcast/psum | solution.py:29
  253.5 0.3 fusion.15
  254.0 0.8 fusion.8
  254.8 4.4 convolution_convert_fusion
  259.2 24.7 %all_to_all.16 = bf16[128,1,24576]{2,1,0:T(2,128)(2,1)} reshape(bf16[768,4096]{1,0:T(8,128)(2,1)} %convolution_convert_fusion) | data formatting | bytes 12582912 | tf_op jit(solution)/shard_map/dispatch/all_to_all | solution.py:48
  284.0 0.5 broadcast.85
  284.5 38.9 %reduce.2 = bf16[128,24576]{1,0:T(8,128)(2,1)} reduce(bf16[128,1,24576]{2,1,0:T(2,128)(2,1)} %all_to_all.16, bf16[]{:T(256)} %broadcast.85), dimensions={1}, to_apply=%all_to_all.16.reduce_sub_computation | reduce | bytes 12582914 | tf_op jit(solution)/shard_map/dispatch/all_to_all | solution.py:48
  323.3 9.4 %reshape.90 = bf16[128,2,12288]{2,1,0:T(2,128)(2,1)} reshape(bf16[128,24576]{1,0:T(8,128)(2,1)} %reduce.2) | data formatting | bytes 12582912
  332.7 83.3 %all_to_all.20 = bf16[128,2,12288]{2,1,0:T(2,128)(2,1)} all-to-all(bf16[128,2,12288]{2,1,0:T(2,128)(2,1)} %reshape.90), channel_id=1, replica_groups=mesh['expert'=64,'dp'=2] {'expert','dp'}, dimensions={0} | all-to-all | bytes 12582912 | tf_op jit(solution)/shard_map/dispatch/all_to_all | solution.py:48
  416.0 33.8 %reshape.91 = bf16[128,1,24576]{2,1,0:T(2,128)(2,1)} reshape(bf16[128,2,12288]{2,1,0:T(2,128)(2,1)} %all_to_all.20) | data formatting | bytes 12582912
  449.8 38.3 %reduce = bf16[128,24576]{1,0:T(8,128)(2,1)} reduce(bf16[128,1,24576]{2,1,0:T(2,128)(2,1)} %reshape.91, bf16[]{:T(256)} %constant.43), dimensions={1}, to_apply=%all_to_all.13.reduce_sub_computation | reduce | bytes 12582914 | tf_op jit(solution)/shard_map/dispatch/all_to_all | solution.py:48
  488.1 11.2 %reshape.86 = bf16[768,4096]{1,0:T(8,128)(2,1)} reshape(bf16[128,24576]{1,0:T(8,128)(2,1)} %reduce) | data formatting | bytes 12582912 | tf_op jit(solution)/shard_map/expert_ffn/reshape | solution.py:50
  499.3 9.1 %fusion.3 = f32[768,768]{1,0:T(8,128)S(1)} fusion(bf16[768,4096]{1,0:T(8,128)(2,1)} %reshape.86, bf16[1,4096,768]{2,1,0:T(8,128)(2,1)} %param.8), kind=kOutput, calls=%fused_computation.8 | convolution fusion | flops 4831838208 | bytes 14942208 | tf_op jit(solution)/shard_map/expert_ffn/dot_general | solution.py:10
  508.5 8.0 %multiply_convert_fusion = bf16[768,768]{1,0:T(8,128)(2,1)S(1)} fusion(f32[768,768]{1,0:T(8,128)S(1)} %fusion.3, bf16[768,4096]{1,0:T(8,128)(2,1)S(1)} %copy-done.1, bf16[1,4096,768]{2,1,0:T(8,128)(2,1)} %param.9), kind=kOutput, calls=%fused_computation.15 | convolution fusion | flops 4835377152 | bytes 16121856 | tf_op jit(solution)/shard_map/expert_ffn/dot_general | solution.py:11
  516.5 7.1 convolution_convert_fusion.1
  523.6 23.8 %all_to_all.17 = bf16[128,1,24576]{2,1,0:T(2,128)(2,1)} reshape(bf16[768,4096]{1,0:T(8,128)(2,1)} %convolution_convert_fusion.1) | data formatting | bytes 12582912 | tf_op jit(solution)/shard_map/return/all_to_all | solution.py:52
  547.3 38.8 %reduce.3 = bf16[128,24576]{1,0:T(8,128)(2,1)} reduce(bf16[128,1,24576]{2,1,0:T(2,128)(2,1)} %all_to_all.17, bf16[]{:T(256)} %broadcast.85), dimensions={1}, to_apply=%all_to_all.17.reduce_sub_computation | reduce | bytes 12582914 | tf_op jit(solution)/shard_map/return/all_to_all | solution.py:52
  586.2 9.4 %reshape.92 = bf16[128,2,12288]{2,1,0:T(2,128)(2,1)} reshape(bf16[128,24576]{1,0:T(8,128)(2,1)} %reduce.3) | data formatting | bytes 12582912
  595.6 6.9 all-to-all-start.1
  602.6 0.8 select_reduce_fusion
  603.4 74.8 %all-to-all-done.1 = bf16[128,2,12288]{2,1,0:T(2,128)(2,1)} async-done(((bf16[128,2,12288]{2,1,0:T(2,128)(2,1)}), bf16[128,2,12288]{2,1,0:T(2,128)(2,1)}, u32[]{:S(2)}, u32[]{:S(2)}) %all-to-all-start.1) | async-done | bytes 6291488 | tf_op jit(solution)/shard_map/return/all_to_all | solution.py:52
  678.2 33.8 %reshape.93 = bf16[128,1,24576]{2,1,0:T(2,128)(2,1)} reshape(bf16[128,2,12288]{2,1,0:T(2,128)(2,1)} %all-to-all-done.1) | data formatting | bytes 12582912
  712.0 38.3 %reduce.1 = bf16[128,24576]{1,0:T(8,128)(2,1)} reduce(bf16[128,1,24576]{2,1,0:T(2,128)(2,1)} %reshape.93, bf16[]{:T(256)} %constant.43), dimensions={1}, to_apply=%all_to_all.15.reduce_sub_computation | reduce | bytes 12582914 | tf_op jit(solution)/shard_map/return/all_to_all | solution.py:52
  750.3 11.1 %reshape.87 = bf16[768,4096]{1,0:T(8,128)(2,1)} reshape(bf16[128,24576]{1,0:T(8,128)(2,1)} %reduce.1) | data formatting | bytes 12582912 | tf_op jit(solution)/shard_map/return/reshape | solution.py:55
  761.4 3.9 convolution_bitcast_fusion.1
  765.3 7.2 fusion.7
  772.5 6.8 fusion.5
  (30 shorter events, 0.9 us)
Async XLA Ops:
  6.5 248.3 %copy-start = (bf16[96,4096]{1,0:T(8,128)(2,1)S(1)}, bf16[96,4096]{1,0:T(8,128)(2,1)}, u32[]{:S(2)}) copy-start(bf16[96,4096]{1,0:T(8,128)(2,1)} %param.7) | copy-start | bytes 2359300
  6.5 246.7 %all-reduce.5.cloned.1.call-start = ((), (), s32[]{:S(2)}) async-start(), calls=%async_computation.2 | async-start | bytes 37748736 | tf_op jit(solution)/shard_map/hot_weight_broadcast/psum | solution.py:29
  23.1 0.7 copy-start.2
  23.2 738.2 %all-reduce.7.cloned.1.call-start = ((), (), s32[]{:S(2)}) async-start(), calls=%async_computation.3 | async-start | bytes 37748736 | tf_op jit(solution)/shard_map/hot_weight_broadcast/psum | solution.py:29
  488.1 28.4 %slice-start = ((s8[6291456]{0:T(1024)(128)(4,1)}), s8[2097152]{0:T(1024)(128)(4,1)S(1)}, s32[]{:S(2)}) async-start(s8[6291456]{0:T(1024)(128)(4,1)} %bitcast.49), calls=%async_computation.4 | async-start | bytes 4194304
  499.3 9.1 %copy-start.1 = (bf16[768,4096]{1,0:T(8,128)(2,1)S(1)}, bf16[768,4096]{1,0:T(8,128)(2,1)}, u32[]{:S(2)}) copy-start(bf16[768,4096]{1,0:T(8,128)(2,1)} %reshape.86) | copy-start | bytes 18874372
  499.3 17.1 %slice-start.1 = ((s8[6291456]{0:T(1024)(128)(4,1)}), s8[4194304]{0:T(1024)(128)(4,1)S(1)}, s32[]{:S(2)}) async-start(s8[6291456]{0:T(1024)(128)(4,1)} %bitcast.49), calls=%async_computation.5 | async-start | bytes 8388608
  595.6 6.9 copy-start.3
  595.6 82.6 %all-to-all-start.1 = ((bf16[128,2,12288]{2,1,0:T(2,128)(2,1)}), bf16[128,2,12288]{2,1,0:T(2,128)(2,1)}, u32[]{:S(2)}, u32[]{:S(2)}) async-start(bf16[128,2,12288]{2,1,0:T(2,128)(2,1)} %reshape.92), calls=%async_computation.1 | async-start | bytes 12582912 | tf_op jit(solution)/shard_map/return/all_to_all | solution.py:52
Sparse Core Ops, SparseCore 0:
  23.3 229.8 all-reduce.4
  256.3 67.5 all-reduce.6
